TPU v7x, 32 devices: a whole 2x2x4 slice. The times are simulated.
32 devices in a mesh: gx: 8 (over y, x, core), wa: 4 (over z).
Axes of the slice: x: 2, y: 2, z: 4, core: 2. Of those that a mesh axis runs over, the one named last changes fastest.
Arguments:
- feats: bfloat16 [8, 16, 8, 8, 8, 256], P('gx', 'wa'), may hold values from -6 to 6
- brick_ids: int32 [8, 16], P('gx', 'wa'), may hold values from 0 to 16, as said below
- conv3_w: bfloat16 [27, 256, 256], replicated, may hold values from -0.078125 to 0.078125
- conv3_scale: float32 [256], replicated, may hold values from 0.5 to 2
- conv3_bias: float32 [256], replicated, may hold values from -0.5 to 0.5
- bev_gain: float32 [256], replicated, may hold values from 0.5 to 2
- conv2_w: bfloat16 [9, 256, 256], replicated, may hold values from -0.125 to 0.125
- conv2_scale: float32 [256], replicated, may hold values from 0.5 to 2
- conv2_bias: float32 [256], replicated, may hold values from -0.5 to 0.5
Outputs:
- bev_out: bfloat16 [64, 128, 256], P('gx', 'wa')
Inputs may be any that keep to these rules, and one draw needn't show every extreme that they name: `brick_ids`: for each g and each w < 4 / 2, slabs (g, w) and (g, w + 4 / 2) list exactly 4 occupied bricks together: slab w in its first k slots and slab w + 4 / 2 in its last 4 - k slots, with 1 <= k <= 3; the remaining slots hold 16; the bricks listed by one slab are distinct.
All inputs are finite; a program needn't handle non-finite values.
Results may differ from a plain program's by a relative error of at most 0.01.
Values may be sent and summed in bfloat16 or wider, within the bound.
A program may use at most 128 MiB of HBM per device.

v0:
```python
import jax
import jax.numpy as jnp
from jax import lax
from jax.sharding import PartitionSpec as P

BY = 16


def extended_2(block, sides, width):
    for axis, dim in sides:
        count = lax.axis_size(axis)
        forward = [(i, i + 1) for i in range(count - 1)]
        backward = [(target, source) for source, target in forward]
        low = lax.ppermute(
            lax.slice_in_dim(block, block.shape[dim] - width, None, axis=dim), axis, forward
        )
        high = lax.ppermute(lax.slice_in_dim(block, 0, width, axis=dim), axis, backward)
        block = jnp.concatenate([low, block, high], axis=dim)
    return block


def conv_volume(padded_tiles, weights, brick_edge):
    channels = padded_tiles.shape[-1]
    summed = jnp.zeros((padded_tiles.shape[0] * brick_edge**3, channels), jnp.float32)
    for offset in range(27):
        shift_x, shift_y, shift_z = (offset // 9, offset // 3 % 3, offset % 3)
        window = padded_tiles[
            :,
            shift_x : shift_x + brick_edge,
            shift_y : shift_y + brick_edge,
            shift_z : shift_z + brick_edge,
        ]
        summed = summed + jnp.dot(
            window.reshape(-1, channels), weights[offset], preferred_element_type=jnp.float32
        )
    return summed.reshape(padded_tiles.shape[0], brick_edge, brick_edge, brick_edge, channels)


def brick_block(padded_tiles, weights, conv_scale, conv_bias, brick_edge):
    conv_out = conv_volume(padded_tiles, weights, brick_edge)
    center = padded_tiles[:, 1 : brick_edge + 1, 1 : brick_edge + 1, 1 : brick_edge + 1].astype(
        jnp.float32
    )
    return jax.nn.relu(conv_out * conv_scale + conv_bias + center).astype(jnp.bfloat16)


def rms_norm(plane, gain_vec):
    mean_sq = jnp.mean(plane * plane, axis=-1, keepdims=True)
    return (plane / jnp.sqrt(mean_sq + 1e-05) * gain_vec).astype(jnp.bfloat16)


def plane_block(normed_pad, weights, conv_scale, conv_bias, residual):
    rows_x, rows_y, channels = residual.shape
    summed = jnp.zeros((rows_x * rows_y, channels), jnp.float32)
    for offset in range(9):
        shift_x, shift_y = (offset // 3, offset % 3)
        window = normed_pad[shift_x : shift_x + rows_x, shift_y : shift_y + rows_y].reshape(
            -1, channels
        )
        summed = summed + jnp.dot(window, weights[offset], preferred_element_type=jnp.float32)
    summed = summed.reshape(rows_x, rows_y, channels)
    return (jax.nn.relu(summed * conv_scale + conv_bias) + residual.astype(jnp.float32)).astype(
        jnp.bfloat16
    )


def per_device(
    feats, brick_ids, conv3_w, conv3_scale, conv3_bias, bev_gain, conv2_w, conv2_scale, conv2_bias
):
    brick_edge = feats.shape[2]
    channels = feats.shape[-1]
    slots = feats.shape[1]
    listed = brick_ids[0]
    tiles = feats[0]
    is_live = listed < BY
    placing = (jnp.arange(BY, dtype=jnp.int32)[:, None] == listed[None, :]).astype(jnp.bfloat16)
    filled = jnp.dot(placing, tiles.reshape(slots, -1), preferred_element_type=jnp.float32).astype(
        jnp.bfloat16
    )
    filled = filled.reshape(BY, brick_edge, brick_edge, brick_edge, channels).transpose(
        1, 0, 2, 3, 4
    )
    filled = filled.reshape(brick_edge, BY * brick_edge, brick_edge, channels)
    extended = extended_2(filled, (("gx", 0), ("wa", 2)), 1)
    extended = jnp.pad(extended, ((0, 0), (1, 1), (0, 0), (0, 0)))
    box_size = brick_edge + 2

    def cut_region(brick_y):
        zero_index = jnp.zeros((), jnp.int32)
        start_y = brick_y * brick_edge
        return lax.dynamic_slice(
            extended,
            (zero_index, start_y, zero_index, zero_index),
            (box_size, box_size, box_size, channels),
        )

    regions = jax.vmap(cut_region)(listed)
    blocks = brick_block(regions, conv3_w, conv3_scale, conv3_bias, brick_edge)
    columns = jnp.sum(blocks.astype(jnp.float32), axis=3) * is_live[:, None, None, None].astype(
        jnp.float32
    )
    plane = jnp.dot(
        placing.astype(jnp.float32), columns.reshape(slots, -1), precision=lax.Precision.HIGHEST
    )
    plane = plane.reshape(BY, brick_edge, brick_edge, channels).transpose(1, 0, 2, 3)
    plane = plane.reshape(brick_edge, BY * brick_edge, channels)
    owned = lax.psum_scatter(
        plane.astype(jnp.bfloat16), "wa", scatter_dimension=1, tiled=True
    ).astype(jnp.float32)
    normed = rms_norm(owned, bev_gain)
    normed_pad = extended_2(normed, (("gx", 0), ("wa", 1)), 1)
    return plane_block(normed_pad, conv2_w, conv2_scale, conv2_bias, normed)


def solution(mesh):
    return jax.shard_map(
        per_device,
        mesh=mesh,
        in_specs=(
            P("gx", "wa", None, None, None, None),
            P("gx", "wa"),
            P(),
            P(),
            P(),
            P(),
            P(),
            P(),
            P(),
        ),
        out_specs=P("gx", "wa", None),
        check_vma=False,
    )
```

profile of v0, /device:TPU:1, one launch (start us, length us, event | category | flops | bytes accessed | tf_op | source)
XLA Modules:
  0.0 166.7 jit_solution(2028455756248816963)
XLA Ops:
  6.5 2.0 %reshape_squeeze.3 = bf16[4,131072]{1,0:T(4,128)(2,1)S(1)} reshape(bf16[1,4,8,8,8,256]{5,4,3,2,1,0:T(8,128)(2,1)} %param.9) | data formatting | bytes 2097152 | tf_op jit(solution)/shard_map/reshape;squeeze | solution.py:77
  8.6 1.7 %convolution_convert_fusion = bf16[16,131072]{1,0:T(8,128)(2,1)S(1)} fusion(bf16[4,131072]{1,0:T(4,128)(2,1)S(1)} %reshape_squeeze.3, s32[4]{0:T(128)S(1)} %bitcast.267), kind=kOutput, calls=%fused_computation.1 | convolution fusion | flops 18874432 | bytes 5242896 | tf_op jit(solution)/shard_map/dot_general | solution.py:77
  11.3 4.5 %collective-permute-start = (bf16[1,128,8,256]{3,2,0,1:T(8,128)(2,1)S(1)}, bf16[1,128,8,256]{3,2,0,1:T(8,128)(2,1)S(1)}, u32[]{:S(2)}, u32[]{:S(2)}) collective-permute-start(bf16[1,128,8,256]{3,2,0,1:T(8,128)(2,1)S(1)} %bitcast.265), channel_id=1, source_target_pairs={{0,4},{4,8},{8,12},{12,16},{16,20},{20,24},{24,28},{1,5},{5,9},{9,... | collective-permute-start | bytes 1572872 | tf_op jit(solution)/shard_map/ppermute | solution.py:14
  15.8 1.9 %collective-permute-start.1 = (bf16[1,128,8,256]{3,2,0,1:T(8,128)(2,1)S(1)}, bf16[1,128,8,256]{3,2,0,1:T(8,128)(2,1)S(1)}, u32[]{:S(2)}, u32[]{:S(2)}) collective-permute-start(bf16[1,128,8,256]{3,2,0,1:T(8,128)(2,1)S(1)} %bitcast.264), channel_id=1, source_target_pairs={{4,0},{8,4},{12,8},{16,12},{20,16},{24,20},{28,24},{5,1},{9,5},{13... | collective-permute-start | bytes 1572872 | tf_op jit(solution)/shard_map/ppermute | solution.py:17
  18.3 3.6 %collective-permute-done = bf16[1,128,8,256]{3,2,0,1:T(8,128)(2,1)S(1)} collective-permute-done((bf16[1,128,8,256]{3,2,0,1:T(8,128)(2,1)S(1)}, bf16[1,128,8,256]{3,2,0,1:T(8,128)(2,1)S(1)}, u32[]{:S(2)}, u32[]{:S(2)}) %collective-permute-start) | collective-permute-done | bytes 524320 | tf_op jit(solution)/shard_map/ppermute | solution.py:14
  21.9 7.3 %collective-permute-done.1 = bf16[1,128,8,256]{3,2,0,1:T(8,128)(2,1)S(1)} collective-permute-done((bf16[1,128,8,256]{3,2,0,1:T(8,128)(2,1)S(1)}, bf16[1,128,8,256]{3,2,0,1:T(8,128)(2,1)S(1)}, u32[]{:S(2)}, u32[]{:S(2)}) %collective-permute-start.1) | collective-permute-done | bytes 524320 | tf_op jit(solution)/shard_map/ppermute | solution.py:17
  29.2 2.2 %pad_maximum_fusion.2 = (bf16[10,128,1,256]{3,2,0,1:T(2,128)(2,1)S(1)}, bf16[10,128,1,256]{3,2,0,1:T(2,128)(2,1)S(1)}) fusion(bf16[1,128,8,256]{3,2,0,1:T(8,128)(2,1)S(1)} %collective-permute-done.1, bf16[8,128,8,256]{3,2,0,1:T(8,128)(2,1)S(1)} %bitcast.218, bf16[1,128,8,256]{3,2,0,1:T(8,128)(2,1)S(1)} %collective-permute-done), kind=kLoop, calls=%fused_computation.46 | loop fusion | flops 3932160 | bytes 6553600 | tf_op jit(solution)/shard_map/slice | solution.py:15
  31.5 3.5 %collective-permute-start.2 = (bf16[10,128,1,256]{3,1,2,0:T(8,128)(2,1)S(1)}, bf16[10,128,1,256]{3,1,2,0:T(8,128)(2,1)S(1)}, u32[]{:S(2)}, u32[]{:S(2)}) collective-permute-start(bf16[10,128,1,256]{3,1,2,0:T(8,128)(2,1)S(1)} %copy.77), channel_id=1, source_target_pairs={{0,1},{1,2},{2,3},{4,5},{5,6},{6,7},{8,9},{9,10},{10,11},{12,13},{... | collective-permute-start | bytes 1966088 | tf_op jit(solution)/shard_map/ppermute | solution.py:14
  35.2 1.5 collective-permute-start.3
  36.7 5.8 %collective-permute-done.2 = bf16[10,128,1,256]{3,1,2,0:T(8,128)(2,1)S(1)} collective-permute-done((bf16[10,128,1,256]{3,1,2,0:T(8,128)(2,1)S(1)}, bf16[10,128,1,256]{3,1,2,0:T(8,128)(2,1)S(1)}, u32[]{:S(2)}, u32[]{:S(2)}) %collective-permute-start.2) | collective-permute-done | bytes 655392 | tf_op jit(solution)/shard_map/ppermute | solution.py:14
  43.5 3.0 %collective-permute-done.3 = bf16[10,128,1,256]{3,1,2,0:T(8,128)(2,1)S(1)} collective-permute-done((bf16[10,128,1,256]{3,1,2,0:T(8,128)(2,1)S(1)}, bf16[10,128,1,256]{3,1,2,0:T(8,128)(2,1)S(1)}, u32[]{:S(2)}, u32[]{:S(2)}) %collective-permute-start.3) | collective-permute-done | bytes 655392 | tf_op jit(solution)/shard_map/ppermute | solution.py:17
  47.5 15.1 %select_maximum_fusion = bf16[10,130,10,256]{3,2,0,1:T(8,128)(2,1)} fusion(bf16[10,128,1,256]{3,2,0,1:T(2,128)(2,1)S(1)} %copy.80, bf16[10,128,1,256]{3,2,0,1:T(2,128)(2,1)S(1)} %copy.79, bf16[1,128,8,256]{3,2,0,1:T(8,128)(2,1)S(1)} %collective-permute-done.1, bf16[8,128,8,256]{3,2,0,1:T(8,128)(2,1)S(1)} %bitcast.219, ...), kind=kLoop, calls=%fused_computation.5 | loop fusion | flops 59904000 | bytes 13209600 | tf_op jit(solution)/shard_map/concatenate | solution.py:18
  62.6 4.8 %gather_fusion = bf16[4,10,10,10,256]{4,3,1,2,0:T(8,128)(2,1)S(1)} fusion(bf16[10,130,10,256]{3,2,0,1:T(8,128)(2,1)} %select_maximum_fusion, s32[4]{0:T(128)S(1)} %fusion.96), kind=kCustom, calls=%fused_computation | custom fusion | bytes 4096064 | tf_op jit(solution)/shard_map/vmap()/gather | solution.py:91
  67.4 3.7 %fusion.99 = (bf16[4,8,8,8,256]{4,3,1,2,0:T(8,128)(2,1)}, bf16[4,8,8,8,256]{4,3,1,2,0:T(8,128)(2,1)}, bf16[4,8,8,8,256]{4,3,1,2,0:T(8,128)(2,1)}, bf16[4,8,8,8,2...) fusion(bf16[4,10,10,10,256]{4,3,1,2,0:T(8,128)(2,1)S(1)} %gathe, ...), kind=kLoop, calls=%fused_computation.160 | loop fusion | bytes 16777216 | tf_op jit(solution)/shard_map/slice | solution.py:27
  71.2 7.8 %fusion.98 = (bf16[4,8,8,8,256]{4,3,1,2,0:T(8,128)(2,1)}, bf16[4,8,8,8,256]{4,3,1,2,0:T(8,128)(2,1)}, bf16[4,8,8,8,256]{4,3,1,2,0:T(8,128)(2,1)}, bf16[4,8,8,8,2...) fusion(bf16[4,10,10,10,256]{4,3,1,2,0:T(8,128)(2,1)S(1)} %gathe, ...), kind=kLoop, calls=%fused_computation.159 | loop fusion | bytes 39845888 | tf_op jit(solution)/shard_map/slice | solution.py:27
  79.0 1.5 copy.81
  96.6 1.6 copy-done.26
  110.3 1.4 convert_reduce_fusion
  113.9 25.3 %reduce-scatter.2.cloned.1.call-done = bf16[8,32,256]{2,1,0:T(8,128)(2,1)} async-done(((bf16[8,128,256]{2,1,0:T(8,128)(2,1)}), bf16[8,32,256]{2,1,0:T(8,128)(2,1)}) %reduce-scatter.2.cloned.1.call-update) | async-done | bytes 131088 | tf_op jit(solution)/shard_map/reduce_scatter | solution.py:107
  141.2 5.2 %collective-permute-start.4 = (bf16[1,32,256]{2,1,0:T(8,128)(2,1)S(1)}, bf16[1,32,256]{2,1,0:T(8,128)(2,1)S(1)}, u32[]{:S(2)}, u32[]{:S(2)}) collective-permute-start(bf16[1,32,256]{2,1,0:T(8,128)(2,1)S(1)} %get-tuple-element.48), channel_id=1, source_target_pairs={{0,4},{4,8},{8,12},{12,16},{16,20},{20,24},{24,28},{1,5},{5,9},{9,... | collective-permute-start | bytes 49160 | tf_op jit(solution)/shard_map/ppermute | solution.py:14
  146.5 1.9 %collective-permute-start.5 = (bf16[1,32,256]{2,1,0:T(8,128)(2,1)S(1)}, bf16[1,32,256]{2,1,0:T(8,128)(2,1)S(1)}, u32[]{:S(2)}, u32[]{:S(2)}) collective-permute-start(bf16[1,32,256]{2,1,0:T(8,128)(2,1)S(1)} %get-tuple-element.49), channel_id=1, source_target_pairs={{4,0},{8,4},{12,8},{16,12},{20,16},{24,20},{28,24},{5,1},{9,5},{13... | collective-permute-start | bytes 49160 | tf_op jit(solution)/shard_map/ppermute | solution.py:17
  148.4 3.1 %collective-permute-done.5 = bf16[1,32,256]{2,1,0:T(8,128)(2,1)S(1)} collective-permute-done((bf16[1,32,256]{2,1,0:T(8,128)(2,1)S(1)}, bf16[1,32,256]{2,1,0:T(8,128)(2,1)S(1)}, u32[]{:S(2)}, u32[]{:S(2)}) %collective-permute-start.5) | collective-permute-done | bytes 16416 | tf_op jit(solution)/shard_map/ppermute | solution.py:17
  152.8 1.3 collective-permute-start.7
  154.4 2.9 %collective-permute-done.7 = bf16[10,1,256]{2,1,0:T(2,128)(2,1)S(1)} collective-permute-done((bf16[10,1,256]{2,1,0:T(2,128)(2,1)S(1)}, bf16[10,1,256]{2,1,0:T(2,128)(2,1)S(1)}, u32[]{:S(2)}, u32[]{:S(2)}) %collective-permute-start.7) | collective-permute-done | bytes 5152 | tf_op jit(solution)/shard_map/ppermute | solution.py:17
  (159 shorter events, 39.7 us)
Async XLA Ops:
  6.5 2.0 %copy-start.30 = (s32[1,4]{1,0:T(1,128)S(1)}, s32[1,4]{1,0:T(1,128)}, u32[]{:S(2)}) copy-start(s32[1,4]{1,0:T(1,128)} %param.10) | copy-start | bytes 52
  6.5 132.6 %reduce-scatter.2.cloned.1.call-start = ((), (), s32[]{:S(2)}) async-start(), calls=%async_computation.1 | async-start | bytes 655360 | tf_op jit(solution)/shard_map/reduce_scatter | solution.py:107
  11.3 10.6 %collective-permute-start = (bf16[1,128,8,256]{3,2,0,1:T(8,128)(2,1)S(1)}, bf16[1,128,8,256]{3,2,0,1:T(8,128)(2,1)S(1)}, u32[]{:S(2)}, u32[]{:S(2)}) collective-permute-start(bf16[1,128,8,256]{3,2,0,1:T(8,128)(2,1)S(1)} %bitcast.265), channel_id=1, source_target_pairs={{0,4},{4,8},{8,12},{12,16},{16,20},{20,24},{24,28},{1,5},{5,9},{9,... | collective-permute-start | bytes 1572872 | tf_op jit(solution)/shard_map/ppermute | solution.py:14
  15.8 13.4 %collective-permute-start.1 = (bf16[1,128,8,256]{3,2,0,1:T(8,128)(2,1)S(1)}, bf16[1,128,8,256]{3,2,0,1:T(8,128)(2,1)S(1)}, u32[]{:S(2)}, u32[]{:S(2)}) collective-permute-start(bf16[1,128,8,256]{3,2,0,1:T(8,128)(2,1)S(1)} %bitcast.264), channel_id=1, source_target_pairs={{4,0},{8,4},{12,8},{16,12},{20,16},{24,20},{28,24},{5,1},{9,5},{13... | collective-permute-start | bytes 1572872 | tf_op jit(solution)/shard_map/ppermute | solution.py:17
  31.5 11.0 %collective-permute-start.2 = (bf16[10,128,1,256]{3,1,2,0:T(8,128)(2,1)S(1)}, bf16[10,128,1,256]{3,1,2,0:T(8,128)(2,1)S(1)}, u32[]{:S(2)}, u32[]{:S(2)}) collective-permute-start(bf16[10,128,1,256]{3,1,2,0:T(8,128)(2,1)S(1)} %copy.77), channel_id=1, source_target_pairs={{0,1},{1,2},{2,3},{4,5},{5,6},{6,7},{8,9},{9,10},{10,11},{12,13},{... | collective-permute-start | bytes 1966088 | tf_op jit(solution)/shard_map/ppermute | solution.py:14
  35.2 11.3 %collective-permute-start.3 = (bf16[10,128,1,256]{3,1,2,0:T(8,128)(2,1)S(1)}, bf16[10,128,1,256]{3,1,2,0:T(8,128)(2,1)S(1)}, u32[]{:S(2)}, u32[]{:S(2)}) collective-permute-start(bf16[10,128,1,256]{3,1,2,0:T(8,128)(2,1)S(1)} %copy.78), channel_id=1, source_target_pairs={{1,0},{2,1},{3,2},{5,4},{6,5},{7,6},{9,8},{10,9},{11,10},{13,12},{... | collective-permute-start | bytes 1966088 | tf_op jit(solution)/shard_map/ppermute | solution.py:17
  79.0 1.5 copy-start.25
  79.0 1.8 %copy-start.24 = (bf16[4,8,8,8,256]{4,3,1,2,0:T(8,128)(2,1)S(1)}, bf16[4,8,8,8,256]{4,3,1,2,0:T(8,128)(2,1)}, u32[]{:S(2)}) copy-start(bf16[4,8,8,8,256]{4,3,1,2,0:T(8,128)(2,1)} %get-tuple-element.33) | copy-start | bytes 3145732
  80.5 1.3 copy-start.23
  81.8 1.3 copy-start.21
  83.4 1.3 copy-start.18
  84.4 1.3 copy-start.17
  86.0 1.3 copy-start.14
  87.0 1.3 copy-start.13
  88.6 1.3 copy-start.10
  89.6 1.3 copy-start.9
  91.2 1.3 copy-start.6
  96.1 2.1 %copy-start.26 = (bf16[27,256,256]{2,1,0:T(8,128)(2,1)S(1)}, bf16[27,256,256]{2,1,0:T(8,128)(2,1)}, u32[]{:S(2)}) copy-start(bf16[27,256,256]{2,1,0:T(8,128)(2,1)} %param.11) | copy-start | bytes 10616836
  111.7 28.5 %copy-start.29 = (f32[256]{0:T(256)S(1)}, f32[256]{0:T(256)}, u32[]{:S(2)}) copy-start(f32[256]{0:T(256)} %param.14) | copy-start | bytes 3076
  112.0 42.2 %copy-start.28 = (bf16[9,256,256]{2,1,0:T(8,128)(2,1)S(1)}, bf16[9,256,256]{2,1,0:T(8,128)(2,1)}, u32[]{:S(2)}) copy-start(bf16[9,256,256]{2,1,0:T(8,128)(2,1)} %param.15) | copy-start | bytes 3538948
  141.2 7.1 %collective-permute-start.4 = (bf16[1,32,256]{2,1,0:T(8,128)(2,1)S(1)}, bf16[1,32,256]{2,1,0:T(8,128)(2,1)S(1)}, u32[]{:S(2)}, u32[]{:S(2)}) collective-permute-start(bf16[1,32,256]{2,1,0:T(8,128)(2,1)S(1)} %get-tuple-element.48), channel_id=1, source_target_pairs={{0,4},{4,8},{8,12},{12,16},{16,20},{20,24},{24,28},{1,5},{5,9},{9,... | collective-permute-start | bytes 49160 | tf_op jit(solution)/shard_map/ppermute | solution.py:14
  146.5 5.1 %collective-permute-start.5 = (bf16[1,32,256]{2,1,0:T(8,128)(2,1)S(1)}, bf16[1,32,256]{2,1,0:T(8,128)(2,1)S(1)}, u32[]{:S(2)}, u32[]{:S(2)}) collective-permute-start(bf16[1,32,256]{2,1,0:T(8,128)(2,1)S(1)} %get-tuple-element.49), channel_id=1, source_target_pairs={{4,0},{8,4},{12,8},{16,12},{20,16},{24,20},{28,24},{5,1},{9,5},{13... | collective-permute-start | bytes 49160 | tf_op jit(solution)/shard_map/ppermute | solution.py:17
  151.5 2.8 %collective-permute-start.6 = (bf16[10,1,256]{2,1,0:T(2,128)(2,1)S(1)}, bf16[10,1,256]{2,1,0:T(2,128)(2,1)S(1)}, u32[]{:S(2)}, u32[]{:S(2)}) collective-permute-start(bf16[10,1,256]{2,1,0:T(2,128)(2,1)S(1)} %get-tuple-element.44), channel_id=1, source_target_pairs={{0,1},{1,2},{2,3},{4,5},{5,6},{6,7},{8,9},{9,10},{10,11},{12,13},{... | collective-permute-start | bytes 15368 | tf_op jit(solution)/shard_map/ppermute | solution.py:14
  152.8 4.4 %collective-permute-start.7 = (bf16[10,1,256]{2,1,0:T(2,128)(2,1)S(1)}, bf16[10,1,256]{2,1,0:T(2,128)(2,1)S(1)}, u32[]{:S(2)}, u32[]{:S(2)}) collective-permute-start(bf16[10,1,256]{2,1,0:T(2,128)(2,1)S(1)} %get-tuple-element.45), channel_id=1, source_target_pairs={{1,0},{2,1},{3,2},{5,4},{6,5},{7,6},{9,8},{10,9},{11,10},{13,12},{... | collective-permute-start | bytes 15368 | tf_op jit(solution)/shard_map/ppermute | solution.py:17
  (20 other events, 23.8 us)
Sparse Core Ops, SparseCore 0:
  114.0 25.1 reduce-scatter.1
where the time goes:
time: 168 us; the launch traced here: 167 us
  waiting for transfers between devices  51 us (30%)
  local copies, waits for them, and re-layouts  42.7 us (25%)
  other arithmetic  21.7 us (13%)
  starting transfers between devices  21.1 us (13%)
  matrix products  15.8 us (9%)
  between operations  14.2 us (8%)
    reduce_scatter x1, waiting for transfers between devices, per_device(): lax.psum_scatter(plane.astype(jnp.bfloat16), 'wa', scatter_dimension=1, t...  25.3 us
    ppermute x4, waiting for transfers between devices, extended_2(): lax.ppermute(lax.slice_in_dim(block, 0, width, axis=dim), axis, backward)  16.2 us
    slice x29, local copies, waits for them, and re-layouts, conv_volume(): padded_tiles[:, shift_x:shift_x + brick_edge, shift_y:shift_y + brick_edg...  16.2 us
    unnamed x72, local copies, waits for them, and re-layouts  15.7 us
    concatenate x3, other arithmetic, extended_2(): block = jnp.concatenate([low, block, high], axis=dim)  15.2 us
    ppermute x4, starting transfers between devices, extended_2(): lax.ppermute(lax.slice_in_dim(block, block.shape[dim] - width, None, axis...  14.5 us
    dot_general x27, matrix products, conv_volume(): jnp.dot(window.reshape(-1, channels), weights[offset], preferred_element_...  11.7 us
    ppermute x4, waiting for transfers between devices, extended_2(): lax.ppermute(lax.slice_in_dim(block, block.shape[dim] - width, None, axis...  9.45 us
  transfers between devices with their start and end apart: 9, of which 7 were waited for; matrix products, arithmetic and copies ran while one was open for 1% of the time, Pallas kernels for 0%

commit v1 on v0

v1 whole, which is shorter than its diff:
```python
import functools

import jax
import jax.numpy as jnp
from jax import lax
from jax.experimental import pallas as pl
from jax.experimental.pallas import tpu as pltpu
from jax.sharding import PartitionSpec as P

BY = 16
GONE = -99
FAR = -1000
MESH = pl.DeviceIdType.MESH
F32 = jnp.float32
BF16 = jnp.bfloat16


def side(sign):
    return 0 if sign < 0 else 1


def block_kernel(
    ng, nw, live,
    ids_ref, feats_ref, w3_ref, w2_ref, scale3_ref, bias3_ref, gain_ref, scale2_ref, bias2_ref,
    out_ref,
    tiles, vol, zsend, zrecv, xrecv, erecv, idsend, idrecv, zpad, cols_lhs, w3, w2,
    csend, crecv, xedge, plane, lhs2,
    load_sem, id_s, id_r, x_s, x_r, z_s, z_r, e_s, e_r, c_s, c_r,
):
    g = lax.axis_index("gx")
    w = lax.axis_index("wa")
    edge = tiles.shape[1]
    chans = tiles.shape[-1]
    ydev = out_ref.shape[1]
    per_slab = ydev // edge
    first = jnp.where(w < nw // 2, 0, feats_ref.shape[1] - live)

    def has_x(d):
        return jnp.logical_and(g + d >= 0, g + d < ng)

    def has_z(e):
        return jnp.logical_and(w + e >= 0, w + e < nw)

    def present(d, peer):
        return has_x(d) if d else w != peer

    peers = [(d, peer) for d in (0, -1, 1) for peer in range(nw)]

    load = pltpu.make_async_copy(feats_ref.at[0, pl.ds(first, live)], tiles, load_sem.at[0])
    load.start()
    load_w3 = pltpu.make_async_copy(w3_ref, w3, load_sem.at[1])
    load_w3.start()
    load_w2 = pltpu.make_async_copy(w2_ref, w2, load_sem.at[2])
    load_w2.start()

    barrier = pltpu.get_barrier_semaphore()
    for d, peer in peers:
        @pl.when(present(d, peer))
        def _():
            pl.semaphore_signal(barrier, inc=1, device_id=(g + d, peer), device_id_type=MESH)

    own = [ids_ref[0, first + j] for j in range(live)]
    row = lax.broadcasted_iota(jnp.int32, idsend.shape, 0)
    listed = jnp.full(idsend.shape, GONE, jnp.int32)
    for j in range(live):
        listed = jnp.where(row == j, jnp.where(own[j] < BY, own[j], GONE), listed)
    idsend[...] = listed
    idrecv[1, w] = listed
    for d in (-1, 1):
        @pl.when(jnp.logical_not(has_x(d)))
        def _():
            for peer in range(nw):
                idrecv[1 + d, peer] = jnp.full(idsend.shape, GONE, jnp.int32)

    load.wait()
    for s in range(live):
        vol[s, 1 : edge + 1, edge : edge * (edge + 1), :] = (
            tiles[s].astype(F32).reshape(edge, edge * edge, chans)
        )
    for s in range(live):
        for e, z in ((-1, 0), (1, edge - 1)):
            zsend[side(e), s] = tiles[s].astype(F32)[:, :, z, :].astype(BF16)

    count = (1 + has_x(-1).astype(jnp.int32) + has_x(1).astype(jnp.int32)) * nw - 1
    pl.semaphore_wait(barrier, count)

    def id_copy(d, peer):
        return pltpu.make_async_remote_copy(
            src_ref=idsend, dst_ref=idrecv.at[1 - d, w],
            send_sem=id_s.at[1 + d, peer], recv_sem=id_r.at[1 - d, w],
            device_id=(g + d, peer), device_id_type=MESH,
        )

    def id_arrival(d, peer):
        return pltpu.make_async_remote_copy(
            src_ref=idsend, dst_ref=idrecv.at[1 + d, peer],
            send_sem=id_s.at[1 + d, peer], recv_sem=id_r.at[1 + d, peer],
            device_id=(g + d, peer), device_id_type=MESH,
        )

    def x_copy(d, arrival=False):
        to = side(d) if arrival else side(-d)
        return pltpu.make_async_remote_copy(
            src_ref=tiles.at[:, 0 if d < 0 else edge - 1], dst_ref=xrecv.at[to],
            send_sem=x_s.at[side(d)], recv_sem=x_r.at[to],
            device_id=(g + d, w), device_id_type=MESH,
        )

    def z_copy(e, arrival=False):
        to = side(e) if arrival else side(-e)
        return pltpu.make_async_remote_copy(
            src_ref=zsend.at[side(e)], dst_ref=zrecv.at[to],
            send_sem=z_s.at[side(e)], recv_sem=z_r.at[to],
            device_id=(g, w + e), device_id_type=MESH,
        )

    def e_copy(d, e, arrival=False):
        tx, tz = (side(d), side(e)) if arrival else (side(-d), side(-e))
        return pltpu.make_async_remote_copy(
            src_ref=zsend.at[side(e), :, 0 if d < 0 else edge - 1], dst_ref=erecv.at[tx, tz],
            send_sem=e_s.at[side(d), side(e)], recv_sem=e_r.at[tx, tz],
            device_id=(g + d, w + e), device_id_type=MESH,
        )

    for d in (-1, 1):
        @pl.when(has_x(d))
        def _():
            x_copy(d).start()
    for e in (-1, 1):
        @pl.when(has_z(e))
        def _():
            z_copy(e).start()
    for d in (-1, 1):
        for e in (-1, 1):
            @pl.when(jnp.logical_and(has_x(d), has_z(e)))
            def _():
                e_copy(d, e).start()
    for d, peer in peers:
        @pl.when(present(d, peer))
        def _():
            id_copy(d, peer).start()

    def picked(ids, target, shape, value):
        total = jnp.zeros(shape, F32)
        for j in range(live):
            hit = jnp.broadcast_to(ids[j : j + 1].reshape((1,) * (len(shape) - 1) + (chans,)), shape)
            total = jnp.where(hit == target, value(j), total)
        return total

    last = edge * edge
    for s in range(live):
        vol[s, 1 : edge + 1, 0:edge, :] = picked(
            listed, own[s] - 1, (edge, edge, chans), lambda j: vol[j, 1 : edge + 1, last : last + edge, :]
        )
        vol[s, 1 : edge + 1, last + edge : last + 2 * edge, :] = picked(
            listed, own[s] + 1, (edge, edge, chans), lambda j: vol[j, 1 : edge + 1, edge : 2 * edge, :]
        )

    for d, peer in peers:
        @pl.when(present(d, peer))
        def _():
            id_copy(d, peer).wait_send()
            id_arrival(d, peer).wait_recv()
    for d in (-1, 1):
        @pl.when(has_x(d))
        def _():
            x_copy(d).wait_send()
            x_copy(d, True).wait_recv()

    for d in (-1, 1):
        ids = idrecv[1 + d, w]
        px = 0 if d < 0 else edge + 1
        for s in range(live):
            vol[s, px, edge : last + edge, :] = picked(
                ids, own[s], (edge, edge, chans), lambda j: xrecv[side(d), j].astype(F32)
            ).reshape(last, chans)
            vol[s, px, 0:edge, :] = picked(
                ids, own[s] - 1, (edge, chans), lambda j: xrecv[side(d), j, edge - 1].astype(F32)
            )
            vol[s, px, last + edge : last + 2 * edge, :] = picked(
                ids, own[s] + 1, (edge, chans), lambda j: xrecv[side(d), j, 0].astype(F32)
            )

    for e in (-1, 1):
        @pl.when(has_z(e))
        def _():
            z_copy(e).wait_send()
            z_copy(e, True).wait_recv()
    for d in (-1, 1):
        for e in (-1, 1):
            @pl.when(jnp.logical_and(has_x(d), has_z(e)))
            def _():
                e_copy(d, e).wait_send()
                e_copy(d, e, True).wait_recv()

    for e in (-1, 1):
        at = jnp.clip(w + e, 0, nw - 1)
        for s in range(live):
            target = jnp.where(has_z(e), own[s], FAR)
            for d in (0, -1, 1):
                ids = idrecv[1 + d, at]
                if d == 0:
                    where_x = slice(1, edge + 1)
                    shape = (edge, edge, chans)
                    value = lambda j: zrecv[side(e), j].astype(F32)
                else:
                    where_x = slice(0, 1) if d < 0 else slice(edge + 1, edge + 2)
                    shape = (1, edge, chans)
                    value = lambda j: erecv[side(d), side(e), j].astype(F32)[None]
                zpad[s, side(e), where_x, 1 : edge + 1, :] = picked(ids, target, shape, value)
                zpad[s, side(e), where_x, 0:1, :] = picked(ids, target - 1, shape, value)[
                    :, edge - 1 : edge
                ]
                zpad[s, side(e), where_x, edge + 1 : edge + 2, :] = picked(
                    ids, target + 1, shape, value
                )[:, 0:1]

    pad = edge + 2
    half = edge // 2
    reach = half + 2
    zrow = lax.broadcasted_iota(jnp.int32, (pad, edge, chans), 1)

    def build(step, carry):
        s = step // reach
        xl = step % reach
        low, mid, high = [], [], []
        for xh in range(2):
            px = xl + half * xh
            v = vol[s, px].reshape(pad, edge, chans)
            below = jnp.broadcast_to(zpad[s, 0, px, 0:pad, :][:, None, :], (pad, edge, chans))
            above = jnp.broadcast_to(zpad[s, 1, px, 0:pad, :][:, None, :], (pad, edge, chans))
            low.append(jnp.where(zrow == 0, below, pltpu.roll(v, 1, axis=1)))
            mid.append(v)
            high.append(jnp.where(zrow == edge - 1, above, pltpu.roll(v, edge - 1, axis=1)))
        for c, pair in enumerate((low, mid, high)):
            cols_lhs[s, xl, :, :, c * chans : (c + 1) * chans] = jnp.concatenate(
                pair, axis=1
            ).astype(BF16)
        return carry

    lax.fori_loop(0, live * reach, build, 0)

    load_w3.wait()
    rows = edge * edge * edge
    out_row = lax.broadcasted_iota(jnp.int32, (last, rows), 0)
    in_row = lax.broadcasted_iota(jnp.int32, (last, rows), 1)
    in_pair = in_row // edge
    in_y = (in_pair // 2) % edge
    in_x = in_pair // (2 * edge) + half * (in_pair % 2)
    pool = jnp.where(in_x * edge + in_y == out_row, 1.0, 0.0).astype(BF16)

    def conv(s, carry):
        acc = jnp.zeros((rows, chans), F32)
        for a in range(3):
            for b in range(3):
                window = cols_lhs[s, pl.ds(a, half), pl.ds(b, edge)].reshape(rows, 3 * chans)
                acc = acc + jnp.dot(window, w3[3 * a + b], preferred_element_type=F32)
        center = cols_lhs[s, pl.ds(1, half), pl.ds(1, edge), :, chans : 2 * chans]
        block = acc * scale3_ref[...] + bias3_ref[...] + center.reshape(rows, chans).astype(F32)
        block = jnp.maximum(block, 0.0).astype(BF16)
        summed = jnp.dot(pool, block, preferred_element_type=F32)
        live_row = ids_ref[0, first + s]
        keep = jnp.full((last, chans), live_row, jnp.int32) < BY
        summed = jnp.where(keep, summed, 0.0).reshape(edge, edge, chans).astype(BF16)
        csend[s] = summed
        crecv[w, s] = summed
        return carry

    lax.fori_loop(0, live, conv, 0)

    def c_copy(d, peer, arrival=False):
        src = csend if d == 0 else csend.at[:, 0 if d < 0 else edge - 1]
        if arrival:
            dst = crecv.at[peer] if d == 0 else xedge.at[side(d), peer]
            sem = c_r.at[1 + d, peer]
        else:
            dst = crecv.at[w] if d == 0 else xedge.at[side(-d), w]
            sem = c_r.at[1 - d, w]
        return pltpu.make_async_remote_copy(
            src_ref=src, dst_ref=dst, send_sem=c_s.at[1 + d, peer], recv_sem=sem,
            device_id=(g + d, peer), device_id_type=MESH,
        )

    for d, peer in peers:
        @pl.when(present(d, peer))
        def _():
            c_copy(d, peer).start()
    load_w2.wait()
    for d, peer in peers:
        @pl.when(present(d, peer))
        def _():
            c_copy(d, peer).wait_send()
            c_copy(d, peer, True).wait_recv()

    off = edge
    for d in (0, -1, 1):
        where_x = slice(1, edge + 1) if d == 0 else (slice(0, 1) if d < 0 else slice(edge + 1, edge + 2))
        shape = (edge if d == 0 else 1, edge, chans)
        for q in range(-1, per_slab + 1):
            total = jnp.zeros(shape, F32)
            for peer in range(nw):
                ids = idrecv[1 + d, peer]
                for j in range(live):
                    hit = jnp.broadcast_to(ids[j : j + 1].reshape(1, 1, chans), shape)
                    if d == 0:
                        value = crecv[peer, j].astype(F32)
                    else:
                        value = xedge[side(d), peer, j].astype(F32)[None]
                    total = total + jnp.where(hit == w * per_slab + q, value, 0.0)
            scale = lax.rsqrt(jnp.mean(total * total, axis=-1, keepdims=True) + 1e-05)
            normed = total * scale * gain_ref[...].reshape(1, 1, chans)
            begin = off + q * edge
            plane[where_x, begin : begin + edge, :] = normed

    for c in range(3):
        lhs2[:, :, c * chans : (c + 1) * chans] = plane[
            :, off + c - 1 : off + c - 1 + ydev, :
        ].astype(BF16)
    total = jnp.zeros((edge * ydev, chans), F32)
    for a in range(3):
        total = total + jnp.dot(
            lhs2[a : a + edge].reshape(edge * ydev, 3 * chans), w2[a], preferred_element_type=F32
        )
    residual = lhs2[1 : edge + 1, :, chans : 2 * chans].reshape(edge * ydev, chans).astype(F32)
    result = jnp.maximum(total * scale2_ref[...] + bias2_ref[...], 0.0) + residual
    out_ref[...] = result.reshape(edge, ydev, chans).astype(BF16)


def per_device(
    ng, nw,
    feats, brick_ids, conv3_w, conv3_scale, conv3_bias, bev_gain, conv2_w, conv2_scale, conv2_bias,
):
    slots, edge, chans = feats.shape[1], feats.shape[2], feats.shape[-1]
    live = slots - 1
    ydev = BY * edge // nw
    pad = edge + 2
    reach = edge // 2 + 2
    vmem = pl.BlockSpec(memory_space=pltpu.VMEM)
    hbm = pl.BlockSpec(memory_space=pl.ANY)
    dma = pltpu.SemaphoreType.DMA
    return pl.pallas_call(
        functools.partial(block_kernel, ng, nw, live),
        out_shape=jax.ShapeDtypeStruct((edge, ydev, chans), BF16),
        in_specs=[pl.BlockSpec(memory_space=pltpu.SMEM), hbm, hbm, hbm] + [vmem] * 5,
        out_specs=vmem,
        scratch_shapes=[
            pltpu.VMEM((live, edge, edge, edge, chans), BF16),
            pltpu.VMEM((live, pad, pad * edge, chans), F32),
            pltpu.VMEM((2, live, edge, edge, chans), BF16),
            pltpu.VMEM((2, live, edge, edge, chans), BF16),
            pltpu.VMEM((2, live, edge, edge, chans), BF16),
            pltpu.VMEM((2, 2, live, edge, chans), BF16),
            pltpu.VMEM((8, chans), jnp.int32),
            pltpu.VMEM((3, nw, 8, chans), jnp.int32),
            pltpu.VMEM((live, 2, pad, 16, chans), F32),
            pltpu.VMEM((live, reach, pad, 2 * edge, 3 * chans), BF16),
            pltpu.VMEM((9, 3 * chans, chans), BF16),
            pltpu.VMEM((3, 3 * chans, chans), BF16),
            pltpu.VMEM((live, edge, edge, chans), BF16),
            pltpu.VMEM((nw, live, edge, edge, chans), BF16),
            pltpu.VMEM((2, nw, live, edge, chans), BF16),
            pltpu.VMEM((pad, ydev + 2 * edge, chans), F32),
            pltpu.VMEM((pad, ydev, 3 * chans), BF16),
            dma((3,)),
            dma((3, nw)), dma((3, nw)),
            dma((2,)), dma((2,)),
            dma((2,)), dma((2,)),
            dma((2, 2)), dma((2, 2)),
            dma((3, nw)), dma((3, nw)),
        ],
        compiler_params=pltpu.CompilerParams(
            collective_id=0, has_side_effects=True, vmem_limit_bytes=56 << 20
        ),
    )(
        brick_ids,
        feats,
        conv3_w.reshape(9, 3 * chans, chans),
        conv2_w.reshape(3, 3 * chans, chans),
        conv3_scale.reshape(1, chans),
        conv3_bias.reshape(1, chans),
        bev_gain.reshape(1, chans),
        conv2_scale.reshape(1, chans),
        conv2_bias.reshape(1, chans),
    )


def solution(mesh):
    return jax.shard_map(
        functools.partial(per_device, mesh.shape["gx"], mesh.shape["wa"]),
        mesh=mesh,
        in_specs=(
            P("gx", "wa", None, None, None, None),
            P("gx", "wa"),
            P(),
            P(),
            P(),
            P(),
            P(),
            P(),
            P(),
        ),
        out_specs=P("gx", "wa", None),
        check_vma=False,
    )
```

time: 168 us -> 38 us (0.23)
  waiting for transfers between devices: 51 us -> 0 us
  local copies, waits for them, and re-layouts: 42.7 us -> 1.57 us
  Pallas kernels: 0 us -> 36.3 us
  other arithmetic: 21.7 us -> 0 us
  starting transfers between devices: 21.1 us -> 0 us
  matrix products: 15.8 us -> 0 us
  between operations: 14.2 us -> 0.01 us
    pallas_call x0 -> x1, Pallas kernels: none -> 36.3 us  [per_device(): pl.pallas_call(functools.partial(block_kernel, ng, nw, live), out_shape=j...]
    ppermute x8 -> x0, waiting for transfers between devices: 25.7 us -> none  [the longest x4 16.2 us: extended_2(): lax.ppermute(lax.slice_in_dim(block, 0, width, axis=dim), axis, backward)]
    reduce_scatter x1 -> x0, waiting for transfers between devices: 25.3 us -> none  [per_device(): lax.psum_scatter(plane.astype(jnp.bfloat16), 'wa', scatter_dimension=1, t...]
    ppermute x8 -> x0, starting transfers between devices: 21.1 us -> none  [the longest x4 14.5 us: extended_2(): lax.ppermute(lax.slice_in_dim(block, block.shape[dim] - width, None, axis...]
    slice x34 -> x0, local copies, waits for them, and re-layouts: 16.6 us -> none  [the longest x29 16.2 us: conv_volume(): padded_tiles[:, shift_x:shift_x + brick_edge, shift_y:shift_y + brick_edg...]
    dot_general x38 -> x0, matrix products: 15.8 us -> none  [the longest x27 11.7 us: conv_volume(): jnp.dot(window.reshape(-1, channels), weights[offset], preferred_element_...]
    concatenate x4 -> x0, other arithmetic: 15.2 us -> none  [the longest x3 15.2 us: extended_2(): block = jnp.concatenate([low, block, high], axis=dim)]
    unnamed x72 -> x1, local copies, waits for them, and re-layouts: 15.7 us -> 1.57 us
  transfers between devices with their start and end apart: 9 -> 0, of which waited for: 7 -> 0; matrix products, arithmetic and copies ran while one was open for 1% -> 0% of each run, Pallas kernels for 0% -> 0%
where the time goes in v1:
time: 38 us; the launch traced here: 37.8 us
  Pallas kernels  36.3 us (96%)
  local copies, waits for them, and re-layouts  1.57 us (4%)
    pallas_call x1, Pallas kernels, per_device(): pl.pallas_call(functools.partial(block_kernel, ng, nw, live), out_shape=j...  36.3 us
    unnamed x1, local copies, waits for them, and re-layouts  1.57 us

profile of v1, /device:TPU:1, one launch (start us, length us, event | category | flops | bytes accessed | tf_op | source)
XLA Modules:
  0.0 37.8 jit_solution(10163854705824365004)
XLA Ops:
  0.0 36.3 %shard_map.91 = bf16[8,32,256]{2,1,0:T(8,128)(2,1)} custom-call(s32[1,4]{1,0:T(1,128)} %ids_ref.1, bf16[1,4,8,8,8,256]{5,4,3,2,1,0:T(8,128)(2,1)} %feats_ref.1, bf16[9,768,256]{2,1,0:T(8,128)(2,1)} %bitcast.7, bf16[3,768,256]{2,1,0:T(8,128)(2,1)} %bitcast.8, f32[1,256]{1,0:T(1,128)} %bitcast.9, f32[1,256]{1,0:T(1,128)} %bitcast.10, f32[1,256]{1,0:T(1,128)} %bitcast.11, ...), custom_call_target="tpu_custom_call" | custom-call | tf_op jit(solution)/shard_map/pallas_call | solution.py:341
  36.3 1.6 %copy.11 = bf16[8,32,256]{2,1,0:T(8,128)(2,1)} copy(bf16[8,32,256]{2,1,0:T(8,128)(2,1)} %shard_map.91) | data formatting | bytes 262144

commit v2 on v1

--- a/solution.py
+++ b/solution.py
@@ -46,6 +46,12 @@
 
     peers = [(d, peer) for d in (0, -1, 1) for peer in range(nw)]
 
+    def near(d, peer):
+        return jnp.logical_and(present(d, peer), jnp.abs(w - peer) <= 1)
+
+    def far(d, peer):
+        return jnp.logical_and(present(d, peer), jnp.abs(w - peer) > 1)
+
     load = pltpu.make_async_copy(feats_ref.at[0, pl.ds(first, live)], tiles, load_sem.at[0])
     load.start()
     load_w3 = pltpu.make_async_copy(w3_ref, w3, load_sem.at[1])
@@ -122,28 +128,29 @@
             device_id=(g + d, w + e), device_id_type=MESH,
         )
 
-    for d in (-1, 1):
-        @pl.when(has_x(d))
-        def _():
-            x_copy(d).start()
     for e in (-1, 1):
         @pl.when(has_z(e))
         def _():
             z_copy(e).start()
+    for d in (-1, 1):
+        @pl.when(has_x(d))
+        def _():
+            x_copy(d).start()
     for d in (-1, 1):
         for e in (-1, 1):
             @pl.when(jnp.logical_and(has_x(d), has_z(e)))
             def _():
                 e_copy(d, e).start()
     for d, peer in peers:
-        @pl.when(present(d, peer))
+        @pl.when(near(d, peer))
         def _():
             id_copy(d, peer).start()
 
     def picked(ids, target, shape, value):
         total = jnp.zeros(shape, F32)
         for j in range(live):
-            hit = jnp.broadcast_to(ids[j : j + 1].reshape((1,) * (len(shape) - 1) + (chans,)), shape)
+            wide = jnp.concatenate([ids[j : j + 1]] * 2, axis=1)
+            hit = jnp.broadcast_to(wide.reshape((1,) * (len(shape) - 1) + (chans,)), shape)
             total = jnp.where(hit == target, value(j), total)
         return total
 
@@ -157,7 +164,7 @@
         )
 
     for d, peer in peers:
-        @pl.when(present(d, peer))
+        @pl.when(near(d, peer))
         def _():
             id_copy(d, peer).wait_send()
             id_arrival(d, peer).wait_recv()
@@ -240,6 +247,11 @@
 
     lax.fori_loop(0, live * reach, build, 0)
 
+    for d, peer in peers:
+        @pl.when(far(d, peer))
+        def _():
+            id_copy(d, peer).start()
+
     load_w3.wait()
     rows = edge * edge * edge
     out_row = lax.broadcasted_iota(jnp.int32, (last, rows), 0)
@@ -248,6 +260,19 @@
     in_y = (in_pair // 2) % edge
     in_x = in_pair // (2 * edge) + half * (in_pair % 2)
     pool = jnp.where(in_x * edge + in_y == out_row, 1.0, 0.0).astype(BF16)
+
+    def c_copy(d, peer, s, arrival=False):
+        src = csend.at[s] if d == 0 else csend.at[s, 0 if d < 0 else edge - 1]
+        if arrival:
+            dst = crecv.at[peer, s] if d == 0 else xedge.at[side(d), peer, s]
+            sem = c_r.at[1 + d, peer, s]
+        else:
+            dst = crecv.at[w, s] if d == 0 else xedge.at[side(-d), w, s]
+            sem = c_r.at[1 - d, w, s]
+        return pltpu.make_async_remote_copy(
+            src_ref=src, dst_ref=dst, send_sem=c_s.at[1 + d, peer, s], recv_sem=sem,
+            device_id=(g + d, peer), device_id_type=MESH,
+        )
 
     def conv(s, carry):
         acc = jnp.zeros((rows, chans), F32)
@@ -264,33 +289,25 @@
         summed = jnp.where(keep, summed, 0.0).reshape(edge, edge, chans).astype(BF16)
         csend[s] = summed
         crecv[w, s] = summed
+        for d, peer in peers:
+            @pl.when(present(d, peer))
+            def _():
+                c_copy(d, peer, s).start()
         return carry
 
     lax.fori_loop(0, live, conv, 0)
 
-    def c_copy(d, peer, arrival=False):
-        src = csend if d == 0 else csend.at[:, 0 if d < 0 else edge - 1]
-        if arrival:
-            dst = crecv.at[peer] if d == 0 else xedge.at[side(d), peer]
-            sem = c_r.at[1 + d, peer]
-        else:
-            dst = crecv.at[w] if d == 0 else xedge.at[side(-d), w]
-            sem = c_r.at[1 - d, w]
-        return pltpu.make_async_remote_copy(
-            src_ref=src, dst_ref=dst, send_sem=c_s.at[1 + d, peer], recv_sem=sem,
-            device_id=(g + d, peer), device_id_type=MESH,
-        )
-
-    for d, peer in peers:
-        @pl.when(present(d, peer))
-        def _():
-            c_copy(d, peer).start()
     load_w2.wait()
     for d, peer in peers:
-        @pl.when(present(d, peer))
-        def _():
-            c_copy(d, peer).wait_send()
-            c_copy(d, peer, True).wait_recv()
+        @pl.when(far(d, peer))
+        def _():
+            id_copy(d, peer).wait_send()
+            id_arrival(d, peer).wait_recv()
+        for s in range(live):
+            @pl.when(present(d, peer))
+            def _():
+                c_copy(d, peer, s).wait_send()
+                c_copy(d, peer, s, True).wait_recv()
 
     off = edge
     for d in (0, -1, 1):
@@ -301,7 +318,8 @@
             for peer in range(nw):
                 ids = idrecv[1 + d, peer]
                 for j in range(live):
-                    hit = jnp.broadcast_to(ids[j : j + 1].reshape(1, 1, chans), shape)
+                    wide = jnp.concatenate([ids[j : j + 1]] * 2, axis=1)
+                    hit = jnp.broadcast_to(wide.reshape(1, 1, chans), shape)
                     if d == 0:
                         value = crecv[peer, j].astype(F32)
                     else:
@@ -350,8 +368,8 @@
             pltpu.VMEM((2, live, edge, edge, chans), BF16),
             pltpu.VMEM((2, live, edge, edge, chans), BF16),
             pltpu.VMEM((2, 2, live, edge, chans), BF16),
-            pltpu.VMEM((8, chans), jnp.int32),
-            pltpu.VMEM((3, nw, 8, chans), jnp.int32),
+            pltpu.VMEM((8, chans // 2), jnp.int32),
+            pltpu.VMEM((3, nw, 8, chans // 2), jnp.int32),
             pltpu.VMEM((live, 2, pad, 16, chans), F32),
             pltpu.VMEM((live, reach, pad, 2 * edge, 3 * chans), BF16),
             pltpu.VMEM((9, 3 * chans, chans), BF16),
@@ -366,7 +384,7 @@
             dma((2,)), dma((2,)),
             dma((2,)), dma((2,)),
             dma((2, 2)), dma((2, 2)),
-            dma((3, nw)), dma((3, nw)),
+            dma((3, nw, live)), dma((3, nw, live)),
         ],
         compiler_params=pltpu.CompilerParams(
             collective_id=0, has_side_effects=True, vmem_limit_bytes=56 << 20

time: 38 us -> 32.6 us (0.86)
  Pallas kernels: 36.3 us -> 30.8 us
    pallas_call x1, Pallas kernels: 36.3 us -> 30.8 us  [per_device(): pl.pallas_call(functools.partial(block_kernel, ng, nw, live), out_shape=j...]
where the time goes in v2:
time: 32.6 us; the launch traced here: 32.4 us
  Pallas kernels  30.8 us (94%)
  local copies, waits for them, and re-layouts  1.57 us (5%)
    pallas_call x1, Pallas kernels, per_device(): pl.pallas_call(functools.partial(block_kernel, ng, nw, live), out_shape=j...  30.8 us
    unnamed x1, local copies, waits for them, and re-layouts  1.57 us

profile of v2, /device:TPU:1, one launch (start us, length us, event | category | flops | bytes accessed | tf_op | source)
XLA Modules:
  0.0 32.4 jit_solution(5917262664631176752)
XLA Ops:
  0.0 30.8 %shard_map.91 = bf16[8,32,256]{2,1,0:T(8,128)(2,1)} custom-call(s32[1,4]{1,0:T(1,128)} %ids_ref.1, bf16[1,4,8,8,8,256]{5,4,3,2,1,0:T(8,128)(2,1)} %feats_ref.1, bf16[9,768,256]{2,1,0:T(8,128)(2,1)} %bitcast.7, bf16[3,768,256]{2,1,0:T(8,128)(2,1)} %bitcast.8, f32[1,256]{1,0:T(1,128)} %bitcast.9, f32[1,256]{1,0:T(1,128)} %bitcast.10, f32[1,256]{1,0:T(1,128)} %bitcast.11, ...), custom_call_target="tpu_custom_call" | custom-call | tf_op jit(solution)/shard_map/pallas_call | solution.py:359
  30.9 1.6 %copy.11 = bf16[8,32,256]{2,1,0:T(8,128)(2,1)} copy(bf16[8,32,256]{2,1,0:T(8,128)(2,1)} %shard_map.91) | data formatting | bytes 262144

commit v3 on v2

--- a/solution.py
+++ b/solution.py
@@ -174,20 +174,6 @@
             x_copy(d).wait_send()
             x_copy(d, True).wait_recv()
 
-    for d in (-1, 1):
-        ids = idrecv[1 + d, w]
-        px = 0 if d < 0 else edge + 1
-        for s in range(live):
-            vol[s, px, edge : last + edge, :] = picked(
-                ids, own[s], (edge, edge, chans), lambda j: xrecv[side(d), j].astype(F32)
-            ).reshape(last, chans)
-            vol[s, px, 0:edge, :] = picked(
-                ids, own[s] - 1, (edge, chans), lambda j: xrecv[side(d), j, edge - 1].astype(F32)
-            )
-            vol[s, px, last + edge : last + 2 * edge, :] = picked(
-                ids, own[s] + 1, (edge, chans), lambda j: xrecv[side(d), j, 0].astype(F32)
-            )
-
     for e in (-1, 1):
         @pl.when(has_z(e))
         def _():
@@ -200,10 +186,23 @@
                 e_copy(d, e).wait_send()
                 e_copy(d, e, True).wait_recv()
 
-    for e in (-1, 1):
-        at = jnp.clip(w + e, 0, nw - 1)
-        for s in range(live):
-            target = jnp.where(has_z(e), own[s], FAR)
+    def place(s):
+        mine = ids_ref[0, first + s]
+        for d in (-1, 1):
+            ids = idrecv[1 + d, w]
+            px = 0 if d < 0 else edge + 1
+            vol[s, px, edge : last + edge, :] = picked(
+                ids, mine, (edge, edge, chans), lambda j: xrecv[side(d), j].astype(F32)
+            ).reshape(last, chans)
+            vol[s, px, 0:edge, :] = picked(
+                ids, mine - 1, (edge, chans), lambda j: xrecv[side(d), j, edge - 1].astype(F32)
+            )
+            vol[s, px, last + edge : last + 2 * edge, :] = picked(
+                ids, mine + 1, (edge, chans), lambda j: xrecv[side(d), j, 0].astype(F32)
+            )
+        for e in (-1, 1):
+            at = jnp.clip(w + e, 0, nw - 1)
+            target = jnp.where(has_z(e), mine, FAR)
             for d in (0, -1, 1):
                 ids = idrecv[1 + d, at]
                 if d == 0:
@@ -227,9 +226,7 @@
     reach = half + 2
     zrow = lax.broadcasted_iota(jnp.int32, (pad, edge, chans), 1)
 
-    def build(step, carry):
-        s = step // reach
-        xl = step % reach
+    def build(xl, s):
         low, mid, high = [], [], []
         for xh in range(2):
             px = xl + half * xh
@@ -243,9 +240,7 @@
             cols_lhs[s, xl, :, :, c * chans : (c + 1) * chans] = jnp.concatenate(
                 pair, axis=1
             ).astype(BF16)
-        return carry
-
-    lax.fori_loop(0, live * reach, build, 0)
+        return s
 
     for d, peer in peers:
         @pl.when(far(d, peer))
@@ -253,46 +248,59 @@
             id_copy(d, peer).start()
 
     load_w3.wait()
-    rows = edge * edge * edge
-    out_row = lax.broadcasted_iota(jnp.int32, (last, rows), 0)
-    in_row = lax.broadcasted_iota(jnp.int32, (last, rows), 1)
+    cut = half // 2
+    rows = cut * edge * 2 * edge
+    out_row = lax.broadcasted_iota(jnp.int32, (2 * cut * edge, rows), 0)
+    in_row = lax.broadcasted_iota(jnp.int32, (2 * cut * edge, rows), 1)
     in_pair = in_row // edge
     in_y = (in_pair // 2) % edge
-    in_x = in_pair // (2 * edge) + half * (in_pair % 2)
+    in_x = 2 * (in_pair // (2 * edge)) + in_pair % 2
     pool = jnp.where(in_x * edge + in_y == out_row, 1.0, 0.0).astype(BF16)
 
-    def c_copy(d, peer, s, arrival=False):
-        src = csend.at[s] if d == 0 else csend.at[s, 0 if d < 0 else edge - 1]
+    def c_copy(d, peer, s, h, arrival=False):
+        if d == 0:
+            src, mark = csend.at[s, h], h
+        else:
+            src, mark = csend.at[s, h, 0 if d < 0 else 2 * cut - 1], 0
         if arrival:
-            dst = crecv.at[peer, s] if d == 0 else xedge.at[side(d), peer, s]
-            sem = c_r.at[1 + d, peer, s]
+            dst = crecv.at[peer, s, h] if d == 0 else xedge.at[side(d), peer, s]
+            sem = c_r.at[1 + d, peer, s, mark]
         else:
-            dst = crecv.at[w, s] if d == 0 else xedge.at[side(-d), w, s]
-            sem = c_r.at[1 - d, w, s]
-        return pltpu.make_async_remote_copy(
-            src_ref=src, dst_ref=dst, send_sem=c_s.at[1 + d, peer, s], recv_sem=sem,
+            dst = crecv.at[w, s, h] if d == 0 else xedge.at[side(-d), w, s]
+            sem = c_r.at[1 - d, w, s, mark]
+        return pltpu.make_async_remote_copy(
+            src_ref=src, dst_ref=dst, send_sem=c_s.at[1 + d, peer, s, mark], recv_sem=sem,
             device_id=(g + d, peer), device_id_type=MESH,
         )
 
+    def parts(d):
+        return (0, 1) if d == 0 else ((0,) if d < 0 else (1,))
+
     def conv(s, carry):
-        acc = jnp.zeros((rows, chans), F32)
-        for a in range(3):
-            for b in range(3):
-                window = cols_lhs[s, pl.ds(a, half), pl.ds(b, edge)].reshape(rows, 3 * chans)
-                acc = acc + jnp.dot(window, w3[3 * a + b], preferred_element_type=F32)
-        center = cols_lhs[s, pl.ds(1, half), pl.ds(1, edge), :, chans : 2 * chans]
-        block = acc * scale3_ref[...] + bias3_ref[...] + center.reshape(rows, chans).astype(F32)
-        block = jnp.maximum(block, 0.0).astype(BF16)
-        summed = jnp.dot(pool, block, preferred_element_type=F32)
+        place(s)
+        lax.fori_loop(0, reach, build, s)
         live_row = ids_ref[0, first + s]
-        keep = jnp.full((last, chans), live_row, jnp.int32) < BY
-        summed = jnp.where(keep, summed, 0.0).reshape(edge, edge, chans).astype(BF16)
-        csend[s] = summed
-        crecv[w, s] = summed
-        for d, peer in peers:
-            @pl.when(present(d, peer))
-            def _():
-                c_copy(d, peer, s).start()
+        keep = jnp.full((2 * cut * edge, chans), live_row, jnp.int32) < BY
+        for h in range(2):
+            acc = jnp.zeros((rows, chans), F32)
+            for a in range(3):
+                for b in range(3):
+                    window = cols_lhs[s, pl.ds(a + h * cut, cut), pl.ds(b, edge)]
+                    acc = acc + jnp.dot(
+                        window.reshape(rows, 3 * chans), w3[3 * a + b], preferred_element_type=F32
+                    )
+            center = cols_lhs[s, pl.ds(1 + h * cut, cut), pl.ds(1, edge), :, chans : 2 * chans]
+            block = acc * scale3_ref[...] + bias3_ref[...] + center.reshape(rows, chans).astype(F32)
+            block = jnp.maximum(block, 0.0).astype(BF16)
+            summed = jnp.dot(pool, block, preferred_element_type=F32)
+            summed = jnp.where(keep, summed, 0.0).reshape(2 * cut, edge, chans).astype(BF16)
+            csend[s, h] = summed
+            crecv[w, s, h] = summed
+            for d, peer in peers:
+                if h in parts(d):
+                    @pl.when(present(d, peer))
+                    def _():
+                        c_copy(d, peer, s, h).start()
         return carry
 
     lax.fori_loop(0, live, conv, 0)
@@ -303,15 +311,15 @@
         def _():
             id_copy(d, peer).wait_send()
             id_arrival(d, peer).wait_recv()
-        for s in range(live):
-            @pl.when(present(d, peer))
-            def _():
-                c_copy(d, peer, s).wait_send()
-                c_copy(d, peer, s, True).wait_recv()
+        @pl.when(present(d, peer))
+        def _():
+            for s in range(live):
+                for h in parts(d):
+                    c_copy(d, peer, s, h).wait_send()
+                    c_copy(d, peer, s, h, True).wait_recv()
 
     off = edge
     for d in (0, -1, 1):
-        where_x = slice(1, edge + 1) if d == 0 else (slice(0, 1) if d < 0 else slice(edge + 1, edge + 2))
         shape = (edge if d == 0 else 1, edge, chans)
         for q in range(-1, per_slab + 1):
             total = jnp.zeros(shape, F32)
@@ -321,14 +329,19 @@
                     wide = jnp.concatenate([ids[j : j + 1]] * 2, axis=1)
                     hit = jnp.broadcast_to(wide.reshape(1, 1, chans), shape)
                     if d == 0:
-                        value = crecv[peer, j].astype(F32)
+                        value = crecv[peer, j].reshape(shape).astype(F32)
                     else:
                         value = xedge[side(d), peer, j].astype(F32)[None]
                     total = total + jnp.where(hit == w * per_slab + q, value, 0.0)
             scale = lax.rsqrt(jnp.mean(total * total, axis=-1, keepdims=True) + 1e-05)
             normed = total * scale * gain_ref[...].reshape(1, 1, chans)
             begin = off + q * edge
-            plane[where_x, begin : begin + edge, :] = normed
+            for r in range(shape[0]):
+                if d == 0:
+                    px = 1 + (r // (2 * cut)) * cut + (r % (2 * cut)) // 2 + half * (r % 2)
+                else:
+                    px = 0 if d < 0 else edge + 1
+                plane[px, begin : begin + edge, :] = normed[r]
 
     for c in range(3):
         lhs2[:, :, c * chans : (c + 1) * chans] = plane[
@@ -374,8 +387,8 @@
             pltpu.VMEM((live, reach, pad, 2 * edge, 3 * chans), BF16),
             pltpu.VMEM((9, 3 * chans, chans), BF16),
             pltpu.VMEM((3, 3 * chans, chans), BF16),
-            pltpu.VMEM((live, edge, edge, chans), BF16),
-            pltpu.VMEM((nw, live, edge, edge, chans), BF16),
+            pltpu.VMEM((live, 2, edge // 2, edge, chans), BF16),
+            pltpu.VMEM((nw, live, 2, edge // 2, edge, chans), BF16),
             pltpu.VMEM((2, nw, live, edge, chans), BF16),
             pltpu.VMEM((pad, ydev + 2 * edge, chans), F32),
             pltpu.VMEM((pad, ydev, 3 * chans), BF16),
@@ -384,7 +397,7 @@
             dma((2,)), dma((2,)),
             dma((2,)), dma((2,)),
             dma((2, 2)), dma((2, 2)),
-            dma((3, nw, live)), dma((3, nw, live)),
+            dma((3, nw, live, 2)), dma((3, nw, live, 2)),
         ],
         compiler_params=pltpu.CompilerParams(
             collective_id=0, has_side_effects=True, vmem_limit_bytes=56 << 20

time: 32.6 us -> 34.3 us (1.052); the launches traced: 32.4 us -> 33.7 us
  Pallas kernels: 30.8 us -> 32.1 us
    pallas_call x1, Pallas kernels: 30.8 us -> 32.1 us  [per_device(): pl.pallas_call(functools.partial(block_kernel, ng, nw, live), out_shape=j...]
where the time goes in v3:
time: 34.3 us; the launch traced here: 33.7 us
  Pallas kernels  32.1 us (94%)
  local copies, waits for them, and re-layouts  1.57 us (5%)
    pallas_call x1, Pallas kernels, per_device(): pl.pallas_call(functools.partial(block_kernel, ng, nw, live), out_shape=j...  32.1 us
    unnamed x1, local copies, waits for them, and re-layouts  1.57 us

profile of v3, /device:TPU:1, one launch (start us, length us, event | category | flops | bytes accessed | tf_op | source)
XLA Modules:
  0.0 33.7 jit_solution(17946801159322248441)
XLA Ops:
  0.0 32.1 %shard_map.91 = bf16[8,32,256]{2,1,0:T(8,128)(2,1)} custom-call(s32[1,4]{1,0:T(1,128)} %ids_ref.1, bf16[1,4,8,8,8,256]{5,4,3,2,1,0:T(8,128)(2,1)} %feats_ref.1, bf16[9,768,256]{2,1,0:T(8,128)(2,1)} %bitcast.7, bf16[3,768,256]{2,1,0:T(8,128)(2,1)} %bitcast.8, f32[1,256]{1,0:T(1,128)} %bitcast.9, f32[1,256]{1,0:T(1,128)} %bitcast.10, f32[1,256]{1,0:T(1,128)} %bitcast.11, ...), custom_call_target="tpu_custom_call" | custom-call | tf_op jit(solution)/shard_map/pallas_call | solution.py:372
  32.1 1.6 %copy.11 = bf16[8,32,256]{2,1,0:T(8,128)(2,1)} copy(bf16[8,32,256]{2,1,0:T(8,128)(2,1)} %shard_map.91) | data formatting | bytes 262144

commit v4 on v2

--- a/solution.py
+++ b/solution.py
@@ -174,20 +174,6 @@
             x_copy(d).wait_send()
             x_copy(d, True).wait_recv()
 
-    for d in (-1, 1):
-        ids = idrecv[1 + d, w]
-        px = 0 if d < 0 else edge + 1
-        for s in range(live):
-            vol[s, px, edge : last + edge, :] = picked(
-                ids, own[s], (edge, edge, chans), lambda j: xrecv[side(d), j].astype(F32)
-            ).reshape(last, chans)
-            vol[s, px, 0:edge, :] = picked(
-                ids, own[s] - 1, (edge, chans), lambda j: xrecv[side(d), j, edge - 1].astype(F32)
-            )
-            vol[s, px, last + edge : last + 2 * edge, :] = picked(
-                ids, own[s] + 1, (edge, chans), lambda j: xrecv[side(d), j, 0].astype(F32)
-            )
-
     for e in (-1, 1):
         @pl.when(has_z(e))
         def _():
@@ -200,10 +186,23 @@
                 e_copy(d, e).wait_send()
                 e_copy(d, e, True).wait_recv()
 
-    for e in (-1, 1):
-        at = jnp.clip(w + e, 0, nw - 1)
-        for s in range(live):
-            target = jnp.where(has_z(e), own[s], FAR)
+    def place(s):
+        mine = ids_ref[0, first + s]
+        for d in (-1, 1):
+            ids = idrecv[1 + d, w]
+            px = 0 if d < 0 else edge + 1
+            vol[s, px, edge : last + edge, :] = picked(
+                ids, mine, (edge, edge, chans), lambda j: xrecv[side(d), j].astype(F32)
+            ).reshape(last, chans)
+            vol[s, px, 0:edge, :] = picked(
+                ids, mine - 1, (edge, chans), lambda j: xrecv[side(d), j, edge - 1].astype(F32)
+            )
+            vol[s, px, last + edge : last + 2 * edge, :] = picked(
+                ids, mine + 1, (edge, chans), lambda j: xrecv[side(d), j, 0].astype(F32)
+            )
+        for e in (-1, 1):
+            at = jnp.clip(w + e, 0, nw - 1)
+            target = jnp.where(has_z(e), mine, FAR)
             for d in (0, -1, 1):
                 ids = idrecv[1 + d, at]
                 if d == 0:
@@ -227,9 +226,7 @@
     reach = half + 2
     zrow = lax.broadcasted_iota(jnp.int32, (pad, edge, chans), 1)
 
-    def build(step, carry):
-        s = step // reach
-        xl = step % reach
+    def build(xl, s):
         low, mid, high = [], [], []
         for xh in range(2):
             px = xl + half * xh
@@ -243,9 +240,7 @@
             cols_lhs[s, xl, :, :, c * chans : (c + 1) * chans] = jnp.concatenate(
                 pair, axis=1
             ).astype(BF16)
-        return carry
-
-    lax.fori_loop(0, live * reach, build, 0)
+        return s
 
     for d, peer in peers:
         @pl.when(far(d, peer))
@@ -265,16 +260,18 @@
         src = csend.at[s] if d == 0 else csend.at[s, 0 if d < 0 else edge - 1]
         if arrival:
             dst = crecv.at[peer, s] if d == 0 else xedge.at[side(d), peer, s]
-            sem = c_r.at[1 + d, peer, s]
+            sem = c_r.at[1 + d, peer]
         else:
             dst = crecv.at[w, s] if d == 0 else xedge.at[side(-d), w, s]
-            sem = c_r.at[1 - d, w, s]
-        return pltpu.make_async_remote_copy(
-            src_ref=src, dst_ref=dst, send_sem=c_s.at[1 + d, peer, s], recv_sem=sem,
+            sem = c_r.at[1 - d, w]
+        return pltpu.make_async_remote_copy(
+            src_ref=src, dst_ref=dst, send_sem=c_s.at[1 + d, peer], recv_sem=sem,
             device_id=(g + d, peer), device_id_type=MESH,
         )
 
     def conv(s, carry):
+        place(s)
+        lax.fori_loop(0, reach, build, s)
         acc = jnp.zeros((rows, chans), F32)
         for a in range(3):
             for b in range(3):
@@ -303,11 +300,11 @@
         def _():
             id_copy(d, peer).wait_send()
             id_arrival(d, peer).wait_recv()
-        for s in range(live):
-            @pl.when(present(d, peer))
-            def _():
-                c_copy(d, peer, s).wait_send()
-                c_copy(d, peer, s, True).wait_recv()
+        @pl.when(present(d, peer))
+        def _():
+            every = slice(None)
+            c_copy(d, peer, every).wait_send()
+            c_copy(d, peer, every, True).wait_recv()
 
     off = edge
     for d in (0, -1, 1):
@@ -384,7 +381,7 @@
             dma((2,)), dma((2,)),
             dma((2,)), dma((2,)),
             dma((2, 2)), dma((2, 2)),
-            dma((3, nw, live)), dma((3, nw, live)),
+            dma((3, nw)), dma((3, nw)),
         ],
         compiler_params=pltpu.CompilerParams(
             collective_id=0, has_side_effects=True, vmem_limit_bytes=56 << 20

time: 32.6 us -> 31.1 us (0.954)
  Pallas kernels: 30.8 us -> 29.3 us
    pallas_call x1, Pallas kernels: 30.8 us -> 29.3 us  [per_device(): pl.pallas_call(functools.partial(block_kernel, ng, nw, live), out_shape=j...]
where the time goes in v4:
time: 31.1 us; the launch traced here: 30.9 us
  Pallas kernels  29.3 us (94%)
  local copies, waits for them, and re-layouts  1.57 us (5%)
    pallas_call x1, Pallas kernels, per_device(): pl.pallas_call(functools.partial(block_kernel, ng, nw, live), out_shape=j...  29.3 us
    unnamed x1, local copies, waits for them, and re-layouts  1.57 us

profile of v4, /device:TPU:1, one launch (start us, length us, event | category | flops | bytes accessed | tf_op | source)
XLA Modules:
  0.0 30.9 jit_solution(5151564277983603060)
XLA Ops:
  0.0 29.3 %shard_map.91 = bf16[8,32,256]{2,1,0:T(8,128)(2,1)} custom-call(s32[1,4]{1,0:T(1,128)} %ids_ref.1, bf16[1,4,8,8,8,256]{5,4,3,2,1,0:T(8,128)(2,1)} %feats_ref.1, bf16[9,768,256]{2,1,0:T(8,128)(2,1)} %bitcast.7, bf16[3,768,256]{2,1,0:T(8,128)(2,1)} %bitcast.8, f32[1,256]{1,0:T(1,128)} %bitcast.9, f32[1,256]{1,0:T(1,128)} %bitcast.10, f32[1,256]{1,0:T(1,128)} %bitcast.11, ...), custom_call_target="tpu_custom_call" | custom-call | tf_op jit(solution)/shard_map/pallas_call | solution.py:356
  29.3 1.6 %copy.11 = bf16[8,32,256]{2,1,0:T(8,128)(2,1)} copy(bf16[8,32,256]{2,1,0:T(8,128)(2,1)} %shard_map.91) | data formatting | bytes 262144

commit v5 on v4

--- a/solution.py
+++ b/solution.py
@@ -271,7 +271,7 @@
 
     def conv(s, carry):
         place(s)
-        lax.fori_loop(0, reach, build, s)
+        lax.fori_loop(0, reach, build, s, unroll=2)
         acc = jnp.zeros((rows, chans), F32)
         for a in range(3):
             for b in range(3):
@@ -286,10 +286,15 @@
         summed = jnp.where(keep, summed, 0.0).reshape(edge, edge, chans).astype(BF16)
         csend[s] = summed
         crecv[w, s] = summed
-        for d, peer in peers:
-            @pl.when(present(d, peer))
+        for peer in range(nw):
+            @pl.when(present(0, peer))
             def _():
-                c_copy(d, peer, s).start()
+                c_copy(0, peer, s).start()
+        for d in (-1, 1):
+            @pl.when(has_x(d))
+            def _():
+                for peer in range(nw):
+                    c_copy(d, peer, s).start()
         return carry
 
     lax.fori_loop(0, live, conv, 0)

time: 31.1 us -> 31 us (level)
  no operation moved by 1% of the time
where the time goes in v5:
time: 31 us; the launch traced here: 30.9 us
  Pallas kernels  29.3 us (95%)
  local copies, waits for them, and re-layouts  1.57 us (5%)
    pallas_call x1, Pallas kernels, per_device(): pl.pallas_call(functools.partial(block_kernel, ng, nw, live), out_shape=j...  29.3 us
    unnamed x1, local copies, waits for them, and re-layouts  1.57 us

profile of v5, /device:TPU:1, one launch (start us, length us, event | category | flops | bytes accessed | tf_op | source)
XLA Modules:
  0.0 30.9 jit_solution(10241600066509192189)
XLA Ops:
  0.0 29.3 %shard_map.91 = bf16[8,32,256]{2,1,0:T(8,128)(2,1)} custom-call(s32[1,4]{1,0:T(1,128)} %ids_ref.1, bf16[1,4,8,8,8,256]{5,4,3,2,1,0:T(8,128)(2,1)} %feats_ref.1, bf16[9,768,256]{2,1,0:T(8,128)(2,1)} %bitcast.7, bf16[3,768,256]{2,1,0:T(8,128)(2,1)} %bitcast.8, f32[1,256]{1,0:T(1,128)} %bitcast.9, f32[1,256]{1,0:T(1,128)} %bitcast.10, f32[1,256]{1,0:T(1,128)} %bitcast.11, ...), custom_call_target="tpu_custom_call" | custom-call | tf_op jit(solution)/shard_map/pallas_call | solution.py:361
  29.3 1.6 %copy.11 = bf16[8,32,256]{2,1,0:T(8,128)(2,1)} copy(bf16[8,32,256]{2,1,0:T(8,128)(2,1)} %shard_map.91) | data formatting | bytes 262144
